TPU v7x, 512 devices: a whole 4x4x16 slice. The times are simulated.
512 devices in a mesh: dp: 32 (over y, x, core), mp: 16 (over z).
Axes of the slice: x: 4, y: 4, z: 16, core: 2. Of those that a mesh axis runs over, the one named last changes fastest.
Arguments:
- tokens: bfloat16 [32768, 8192], P('dp', 'mp'), may hold values from -6 to 6
- value_weight: bfloat16 [8192, 1024], P('mp'), may hold values from -0.0625 to 0.0625
- down_panels: bfloat16 [256, 8192, 64], P('dp', 'mp'), may hold values from -0.0625 to 0.0625
- up_panels: bfloat16 [256, 64, 1024], P('dp'), may hold values from -0.75 to 0.75
- cotangent: bfloat16 [32768, 1024], P(('dp', 'mp')), may hold values from -6 to 6
- block_adapter: int32 [256], replicated, may hold values from 0 to 255, as said below
- adapter_slot: int32 [256], replicated, may hold values from 0 to 255, as said below
Outputs:
- projected: bfloat16 [32768, 1024], P(('dp', 'mp'))
- grad_tokens: bfloat16 [32768, 8192], P('dp', 'mp')
- grad_down: bfloat16 [256, 8192, 64], P('dp', 'mp')
- grad_up: bfloat16 [256, 64, 1024], P('dp')
Inputs may be any that keep to these rules, and one draw needn't show every extreme that they name: `block_adapter`: the 8 blocks of one index of dp name adapters stored on 8 different owners, the owner of slot s being s // 8. `adapter_slot`: A permutation of the adapters.
All inputs are finite; a program needn't handle non-finite values.
Results may differ from a plain program's by a relative error of at most 0.005.
Values may be sent and summed in bfloat16 or wider, within the bound.
A program may use at most 128 MiB of HBM per device.

v0:
```python
import jax
import jax.numpy as jnp
from jax import lax
from jax.sharding import PartitionSpec as P

RANK = 64
BLOCK_ROWS = 128


def per_device(
    tokens, value_weight, down_panels, up_panels, cotangent, block_adapter, adapter_slot
):
    n_owners = lax.axis_size("dp")
    myself = lax.axis_index("dp")
    n_split = lax.axis_size("mp")
    my_part = lax.axis_index("mp")
    rows, width_dev = tokens.shape
    own_rows, kv_full = cotangent.shape
    kv_part = kv_full // n_split
    stored = down_panels.shape[0]
    blocks = rows // BLOCK_ROWS
    highest = lax.Precision.HIGHEST
    hits = block_adapter[:, None] == jnp.arange(adapter_slot.shape[0], dtype=jnp.int32)[None, :]
    slots_all = jnp.sum(jnp.where(hits, adapter_slot[None, :], 0), axis=1)
    owner_all = (slots_all // stored).reshape(n_owners, blocks)
    local_all = (slots_all % stored).reshape(n_owners, blocks)
    mine = owner_all == myself
    wanted = jnp.sum(jnp.where(mine, local_all, 0), axis=1)
    served = jnp.any(mine, axis=1)
    pick_mask = (wanted[:, None] == jnp.arange(stored, dtype=jnp.int32)[None, :]) & served[:, None]
    my_owner = lax.dynamic_index_in_dim(owner_all, myself, 0, keepdims=False)
    select_mask = my_owner[:, None] == jnp.arange(n_owners, dtype=jnp.int32)[None, :]
    select_f32 = select_mask.astype(jnp.float32)
    send_a = jnp.take(down_panels, wanted, axis=0)
    up_cols = lax.dynamic_slice_in_dim(up_panels, my_part * kv_part, kv_part, 2)
    send_b = jnp.take(up_cols, wanted, axis=0)
    got_a = lax.all_to_all(send_a, "dp", split_axis=0, concat_axis=0, tiled=True)
    got_b = lax.all_to_all(send_b, "dp", split_axis=0, concat_axis=0, tiled=True)
    panel_a = jnp.take(got_a, my_owner, axis=0)
    panel_b_cols = jnp.take(got_b, my_owner, axis=0)
    first_row = my_part * own_rows
    part_block = jnp.arange(n_split, dtype=jnp.int32) * own_rows // BLOCK_ROWS
    to_parts = jnp.take(panel_b_cols, part_block, axis=0)
    from_parts = lax.all_to_all(to_parts, "mp", split_axis=0, concat_axis=0, tiled=True)
    my_up = from_parts.transpose(1, 0, 2).reshape(RANK, kv_full)
    token_blocks = tokens.reshape(blocks, BLOCK_ROWS, width_dev)
    partial_value = jnp.dot(tokens, value_weight, preferred_element_type=jnp.float32)
    base = lax.psum_scatter(partial_value, "mp", scatter_dimension=0, tiled=True)
    down_part = jnp.einsum(
        "bnd,bdk->bnk", token_blocks, panel_a, preferred_element_type=jnp.float32
    )
    down = lax.psum(down_part, "mp").astype(jnp.bfloat16)
    my_down = lax.dynamic_slice_in_dim(down.reshape(rows, RANK), first_row, own_rows, 0)
    lifted = jnp.dot(my_down, my_up, preferred_element_type=jnp.float32)
    projected = (base + lifted).astype(jnp.bfloat16)
    my_back = jnp.einsum("nc,kc->nk", cotangent, my_up, preferred_element_type=jnp.float32).astype(
        jnp.bfloat16
    )
    back = lax.all_gather(my_back, "mp", axis=0, tiled=True).reshape(blocks, BLOCK_ROWS, RANK)
    cot_all = lax.all_gather(cotangent, "mp", axis=0, tiled=True)
    grad_base = jnp.einsum("nc,dc->nd", cot_all, value_weight, preferred_element_type=jnp.float32)
    through = jnp.einsum("bnk,bdk->bnd", back, panel_a, preferred_element_type=jnp.float32)
    grad_tokens = (grad_base + through.reshape(rows, width_dev)).astype(jnp.bfloat16)
    block_grad_a = jnp.einsum(
        "bnd,bnk->bdk", token_blocks, back, preferred_element_type=jnp.float32
    ).astype(jnp.bfloat16)
    cot_blocks = cot_all.reshape(blocks, BLOCK_ROWS, kv_full)
    cot_share = lax.dynamic_slice_in_dim(cot_blocks, my_part * kv_part, kv_part, 2)
    block_grad_b = jnp.einsum(
        "bnk,bnc->bkc",
        down.reshape(blocks, BLOCK_ROWS, RANK),
        cot_share,
        preferred_element_type=jnp.float32,
    )
    send_ga = jnp.einsum(
        "bo,bdk->odk",
        select_mask.astype(jnp.bfloat16),
        block_grad_a,
        preferred_element_type=jnp.float32,
    ).astype(jnp.bfloat16)
    send_gb = jnp.einsum("bo,bkc->okc", select_f32, block_grad_b, precision=highest)
    recv_ga = lax.all_to_all(send_ga, "dp", split_axis=0, concat_axis=0, tiled=True)
    recv_gb = lax.all_to_all(send_gb, "dp", split_axis=0, concat_axis=0, tiled=True)
    pick_f32 = pick_mask.astype(jnp.float32)
    grad_down = jnp.einsum(
        "ra,rdk->adk", pick_mask.astype(jnp.bfloat16), recv_ga, preferred_element_type=jnp.float32
    ).astype(jnp.bfloat16)
    grad_share = jnp.einsum("ra,rkc->akc", pick_f32, recv_gb, precision=highest).astype(
        jnp.bfloat16
    )
    grad_up = lax.all_gather(grad_share, "mp", axis=2, tiled=True)
    return (projected, grad_tokens, grad_down, grad_up)


def solution(mesh):
    placed = (
        P("dp", "mp"),
        P("mp", None),
        P("dp", "mp", None),
        P("dp", None, None),
        P(("dp", "mp"), None),
        P(),
        P(),
    )
    return jax.shard_map(
        per_device,
        mesh=mesh,
        in_specs=placed,
        out_specs=(P(("dp", "mp"), None), P("dp", "mp"), P("dp", "mp", None), P("dp", None, None)),
        check_vma=False,
    )
```

profile of v0, /device:TPU:4, one launch (start us, length us, event | category | flops | bytes accessed | tf_op | source)
XLA Modules:
  0.0 297.7 jit_solution(200860388559841904)
XLA Ops:
  7.2 0.0 copy-start
  7.2 0.0 all-gather.3.cloned.1.call-start
  7.2 0.7 all-gather.3.cloned.1.call-update
  7.9 0.9 select_reduce_fusion
  8.8 0.1 reduce_sum.23
  8.9 0.1 fusion.43
  9.0 0.1 fusion.18
  9.2 1.7 gather_fusion
  10.9 1.6 broadcast_select_fusion
  12.5 10.2 %all-to-all-start = ((bf16[32,512,64]{1,2,0:T(8,128)(2,1)}), bf16[32,512,64]{1,2,0:T(8,128)(2,1)}, u32[]{:S(2)}, u32[]{:S(2)}) async-start(bf16[32,512,64]{1,2,0:T(8,128)(2,1)} %broadcast_select_fusion), calls=%async_computation.1 | async-start | bytes 4194304 | tf_op jit(solution)/shard_map/all_to_all | solution.py:37
  22.7 0.0 all-gather.5.cloned.1.call-start
  22.8 26.6 %all-to-all-done = bf16[32,512,64]{1,2,0:T(8,128)(2,1)} async-done(((bf16[32,512,64]{1,2,0:T(8,128)(2,1)}), bf16[32,512,64]{1,2,0:T(8,128)(2,1)}, u32[]{:S(2)}, u32[]{:S(2)}) %all-to-all-start) | async-done | bytes 2097184 | tf_op jit(solution)/shard_map/all_to_all | solution.py:37
  49.4 2.2 gather_fusion.1
  51.5 0.0 copy-start.1
  51.6 0.5 convolution_bitcast_fusion
  52.1 62.3 %all-reduce.1 = bf16[8,128,64]{1,2,0:T(8,128)(2,1)S(1)} all-reduce(f32[8,128,64]{1,2,0:T(8,128)S(1)} %convolution_bitcast_fusion), channel_id=1, replica_groups=mesh['dp'=32,'mp'=16] {'mp'}, use_global_device_ids=true, to_apply=%region_3.4 | all-reduce | flops 65536 | bytes 393216 | tf_op jit(solution)/shard_map/psum | solution.py:52
  114.4 0.0 copy-start.3
  114.4 0.0 all-gather.3.cloned.1.call-done
  114.5 1.2 fusion.13
  115.7 0.7 fusion.11
  116.4 0.6 copy.58
  117.1 0.7 reshape.206
  117.7 16.3 %all_to_all.25 = f32[32,1,4096]{2,1,0:T(1,128)S(1)} all-to-all(f32[32,1,4096]{2,1,0:T(1,128)S(1)} %reshape.206), channel_id=1, replica_groups=mesh['dp'=32,'mp'=16] {'dp'}, dimensions={0} | all-to-all | bytes 1048576 | tf_op jit(solution)/shard_map/all_to_all | solution.py:83
  134.0 0.5 broadcast.234
  134.5 1.9 reduce
  136.4 0.4 reshape.207
  136.8 1.0 convolution_convert_fusion.2
  137.9 0.8 copy.60
  138.7 0.0 all-gather.5.cloned.1.call-update
  138.7 0.0 reduce-scatter.2.cloned.1.call-start
  138.7 4.4 %fusion.45 = f32[1024,1024]{1,0:T(8,128)} fusion(bf16[1024,512]{1,0:T(8,128)(2,1)S(1)} %copy-done, bf16[512,1024]{1,0:T(8,128)(2,1)} %param.8), kind=kOutput, calls=%fused_computation.90 | convolution fusion | flops 1073741824 | bytes 6291456 | tf_op jit(solution)/shard_map/dot_general | solution.py:47
  143.2 0.0 reduce-scatter.2.cloned.1.call-update
  143.2 1.0 constant_dynamic-slice_fusion
  144.2 0.6 gather_fusion.2
  144.9 0.1 broadcast_select_fusion.1
  145.0 1.1 reshape.202
  146.1 5.9 %all-to-all-start.1 = ((bf16[32,2,2048]{2,1,0:T(2,128)(2,1)}), bf16[32,2,2048]{2,1,0:T(2,128)(2,1)S(1)}, u32[]{:S(2)}, u32[]{:S(2)}) async-start(bf16[32,2,2048]{2,1,0:T(2,128)(2,1)} %reshape.202), calls=%async_computation.2 | async-start | bytes 524288 | tf_op jit(solution)/shard_map/all_to_all | solution.py:38
  152.0 6.8 %all-to-all-done.1 = bf16[32,2,2048]{2,1,0:T(2,128)(2,1)S(1)} async-done(((bf16[32,2,2048]{2,1,0:T(2,128)(2,1)}), bf16[32,2,2048]{2,1,0:T(2,128)(2,1)S(1)}, u32[]{:S(2)}, u32[]{:S(2)}) %all-to-all-start.1) | async-done | bytes 262176 | tf_op jit(solution)/shard_map/all_to_all | solution.py:38
  158.8 0.4 reshape.203
  159.2 0.6 gather_fusion.3
  159.8 0.1 broadcast_select_fusion.6
  159.8 0.6 gather_fusion.4
  160.5 0.1 broadcast_select_fusion.3
  160.6 0.2 reshape.204
  160.8 22.2 %all_to_all.26 = bf16[16,2,2048]{2,1,0:T(2,128)(2,1)S(1)} all-to-all(bf16[16,2,2048]{2,1,0:T(2,128)(2,1)S(1)} %reshape.204), channel_id=1, replica_groups=mesh['dp'=32,'mp'=16] {'mp'}, dimensions={0} | all-to-all | bytes 262144 | tf_op jit(solution)/shard_map/all_to_all | solution.py:44
  183.0 0.2 reshape.205
  183.2 0.2 copy.48
  183.4 0.2 reshape.156
  183.6 0.2 fusion.8
  183.8 0.1 copy.49
  183.9 30.4 %all_gather.10 = bf16[1024,64]{1,0:T(8,128)(2,1)S(1)} all-gather(bf16[64,64]{1,0:T(8,128)(2,1)S(1)} %copy.49), channel_id=1, replica_groups=mesh['dp'=32,'mp'=16] {'mp'}, dimensions={0}, use_global_device_ids=true | all-gather | bytes 139264 | tf_op jit(solution)/shard_map/all_gather | solution.py:59
  214.2 0.3 fusion.6
  214.6 0.8 convolution_convert_fusion
  215.4 2.5 copy.54
  217.9 6.3 %all-to-all-start.3 = ((bf16[32,512,64]{1,2,0:T(8,128)(2,1)}), bf16[32,512,64]{1,2,0:T(8,128)(2,1)S(1)}, u32[]{:S(2)}, u32[]{:S(2)}) async-start(bf16[32,512,64]{1,2,0:T(8,128)(2,1)} %copy.54), calls=%async_computation.4 | async-start | bytes 4194304 | tf_op jit(solution)/shard_map/all_to_all | solution.py:82
  224.2 1.6 copy_bitcast_fusion
  225.8 2.8 fusion.15
  228.7 22.2 %all-to-all-done.3 = bf16[32,512,64]{1,2,0:T(8,128)(2,1)S(1)} async-done(((bf16[32,512,64]{1,2,0:T(8,128)(2,1)}), bf16[32,512,64]{1,2,0:T(8,128)(2,1)S(1)}, u32[]{:S(2)}, u32[]{:S(2)}) %all-to-all-start.3) | async-done | bytes 2097184 | tf_op jit(solution)/shard_map/all_to_all | solution.py:82
  250.9 1.2 fusion.3
  252.1 1.0 copy.61
  253.1 3.9 %fusion = bf16[1024,512]{1,0:T(8,128)(2,1)} fusion(f32[8,128,512]{2,1,0:T(8,128)S(1)} %copy-done.2, bf16[1024,1024]{1,0:T(8,128)(2,1)} %all-gather.3.cloned.1.call-done, bf16[512,1024]{1,0:T(8,128)(2,1)S(1)} %copy-done.5), kind=kOutput, calls=%fused_computation.6 | convolution fusion | flops 1074790400 | bytes 6291456 | tf_op jit(solution)/shard_map/nc,dc->nd/dot_general | solution.py:61
  256.9 3.3 %copy.62 = bf16[8,64,1024]{2,1,0:T(8,128)(2,1)} copy(bf16[8,64,1024]{1,0,2:T(8,128)(2,1)} %all-gather.5.cloned.1.call-done) | data formatting | bytes 2097152
  260.2 29.0 %reduce-scatter.2.cloned.1.call-done = f32[64,1024]{1,0:T(8,128)} async-done(((f32[1024,1024]{1,0:T(8,128)}), f32[64,1024]{1,0:T(8,128)}) %reduce-scatter.2.cloned.1.call-update) | async-done | bytes 262160 | tf_op jit(solution)/shard_map/reduce_scatter | solution.py:48
  289.3 1.9 fusion.7
  (19 shorter events, 0.1 us)
Async XLA Ops:
  7.2 44.4 %copy-start = (bf16[1024,512]{1,0:T(8,128)(2,1)S(1)}, bf16[1024,512]{1,0:T(8,128)(2,1)}, u32[]{:S(2)}) copy-start(bf16[1024,512]{1,0:T(8,128)(2,1)} %param.7) | copy-start | bytes 3145732
  7.2 107.3 %all-gather.3.cloned.1.call-start = ((), (), s32[]{:S(2)}) async-start(), calls=%async_computation.7 | async-start | bytes 2228224 | tf_op jit(solution)/shard_map/all_gather | solution.py:60
  12.5 36.9 %all-to-all-start = ((bf16[32,512,64]{1,2,0:T(8,128)(2,1)}), bf16[32,512,64]{1,2,0:T(8,128)(2,1)}, u32[]{:S(2)}, u32[]{:S(2)}) async-start(bf16[32,512,64]{1,2,0:T(8,128)(2,1)} %broadcast_select_fusion), calls=%async_computation.1 | async-start | bytes 4194304 | tf_op jit(solution)/shard_map/all_to_all | solution.py:37
  22.7 234.2 %all-gather.5.cloned.1.call-start = ((), (), s32[]{:S(2)}) async-start(), calls=%async_computation.8 | async-start | bytes 2228224 | tf_op jit(solution)/shard_map/all_gather | solution.py:91
  51.5 64.9 %copy-start.1 = (bf16[8,512,64]{1,2,0:T(8,128)(2,1)}, bf16[8,512,64]{1,2,0:T(8,128)(2,1)S(1)}, u32[]{:S(2)}) copy-start(bf16[8,512,64]{1,2,0:T(8,128)(2,1)S(1)} %gather_fusion.1) | copy-start | bytes 1572868
  114.4 1.3 copy-start.3
  138.7 150.6 %reduce-scatter.2.cloned.1.call-start = ((), (), s32[]{:S(2)}) async-start(), calls=%async_computation.6 | async-start | bytes 4456448 | tf_op jit(solution)/shard_map/reduce_scatter | solution.py:48
  146.1 12.7 %all-to-all-start.1 = ((bf16[32,2,2048]{2,1,0:T(2,128)(2,1)}), bf16[32,2,2048]{2,1,0:T(2,128)(2,1)S(1)}, u32[]{:S(2)}, u32[]{:S(2)}) async-start(bf16[32,2,2048]{2,1,0:T(2,128)(2,1)} %reshape.202), calls=%async_computation.2 | async-start | bytes 524288 | tf_op jit(solution)/shard_map/all_to_all | solution.py:38
  152.0 31.6 %copy-start.4 = (bf16[64,1024]{1,0:T(8,128)(2,1)S(1)}, bf16[64,1024]{1,0:T(8,128)(2,1)}, u32[]{:S(2)}) copy-start(bf16[64,1024]{1,0:T(8,128)(2,1)} %param.11) | copy-start | bytes 393220
  217.9 32.9 %all-to-all-start.3 = ((bf16[32,512,64]{1,2,0:T(8,128)(2,1)}), bf16[32,512,64]{1,2,0:T(8,128)(2,1)S(1)}, u32[]{:S(2)}, u32[]{:S(2)}) async-start(bf16[32,512,64]{1,2,0:T(8,128)(2,1)} %copy.54), calls=%async_computation.4 | async-start | bytes 4194304 | tf_op jit(solution)/shard_map/all_to_all | solution.py:82
  250.9 2.2 copy-start.2
  250.9 2.2 copy-start.5
Sparse Core Ops, SparseCore 0:
  10.1 77.7 all-gather.2
  138.8 70.7 all-gather.4
  212.5 76.7 reduce-scatter.1
where the time goes:
time: 298 us
  blocking collectives  131 us (44%)
  waiting for transfers between devices  85.3 us (29%)
  starting transfers between devices  22.5 us (8%)
  local copies, waits for them, and re-layouts  20.6 us (7%)
  matrix products  19.1 us (6%)
  between operations  14.1 us (5%)
  other arithmetic  4.96 us (2%)
    psum x1, blocking collectives, per_device(): down = lax.psum(down_part, 'mp').astype(jnp.bfloat16)  62.3 us
    all_gather x1, blocking collectives, per_device(): lax.all_gather(my_back, 'mp', axis=0, tiled=True)  30.4 us
    reduce_scatter x1, waiting for transfers between devices, per_device(): lax.psum_scatter(partial_value, 'mp', scatter_dimension=0, tiled=True)  29 us
    all_to_all x1, waiting for transfers between devices, per_device(): lax.all_to_all(send_a, 'dp', split_axis=0, concat_axis=0, tiled=True)  26.6 us
    all_to_all x1, waiting for transfers between devices, per_device(): lax.all_to_all(send_ga, 'dp', split_axis=0, concat_axis=0, tiled=True)  22.2 us
    all_to_all x1, blocking collectives, per_device(): lax.all_to_all(to_parts, 'mp', split_axis=0, concat_axis=0, tiled=True)  22.2 us
    all_to_all x1, blocking collectives, per_device(): lax.all_to_all(send_gb, 'dp', split_axis=0, concat_axis=0, tiled=True)  16.3 us
    all_to_all x1, starting transfers between devices, per_device(): lax.all_to_all(send_a, 'dp', split_axis=0, concat_axis=0, tiled=True)  10.2 us
  transfers between devices with their start and end apart: 6, of which 4 were waited for; matrix products, arithmetic and copies ran while one was open for 12% of the time, Pallas kernels for 0%

commit v1 on v0

--- a/solution.py
+++ b/solution.py
@@ -1,3 +1,4 @@
+import functools
 import jax
 import jax.numpy as jnp
 from jax import lax
@@ -5,6 +6,13 @@
 
 RANK = 64
 BLOCK_ROWS = 128
+
+
+def _measure_values(vals, peer_axis):
+    return jnp.sum(lax.all_gather(vals, peer_axis), 0)
+
+
+write_meshes = functools.partial(_measure_values, peer_axis="mp")
 
 
 def per_device(
@@ -49,7 +57,7 @@
     down_part = jnp.einsum(
         "bnd,bdk->bnk", token_blocks, panel_a, preferred_element_type=jnp.float32
     )
-    down = lax.psum(down_part, "mp").astype(jnp.bfloat16)
+    down = write_meshes(down_part).astype(jnp.bfloat16)
     my_down = lax.dynamic_slice_in_dim(down.reshape(rows, RANK), first_row, own_rows, 0)
     lifted = jnp.dot(my_down, my_up, preferred_element_type=jnp.float32)
     projected = (base + lifted).astype(jnp.bfloat16)

time: 298 us -> 373 us (1.25)
  the two profiles are of different devices: /device:TPU:4 before, /device:TPU:2 now
where the time goes in v1:
time: 373 us; the launch traced here: 372 us
  waiting for transfers between devices  215 us (58%)
  blocking collectives  59.6 us (16%)
  starting transfers between devices  29.1 us (8%)
  local copies, waits for them, and re-layouts  23.6 us (6%)
  matrix products  20.4 us (5%)
  between operations  14.1 us (4%)
  other arithmetic  9.46 us (3%)
    all_gather x1, waiting for transfers between devices, per_device(): grad_up = lax.all_gather(grad_share, 'mp', axis=2, tiled=True)  71.6 us
    all_gather x1, waiting for transfers between devices, per_device(): cot_all = lax.all_gather(cotangent, 'mp', axis=0, tiled=True)  68.8 us
    all_gather x1, blocking collectives, per_device(): lax.all_gather(my_back, 'mp', axis=0, tiled=True)  31.7 us
    all_to_all x1, blocking collectives, per_device(): lax.all_to_all(to_parts, 'mp', split_axis=0, concat_axis=0, tiled=True)  27.9 us
    all_to_all x1, waiting for transfers between devices, per_device(): lax.all_to_all(send_a, 'dp', split_axis=0, concat_axis=0, tiled=True)  27.9 us
    reduce_scatter x1, waiting for transfers between devices, per_device(): lax.psum_scatter(partial_value, 'mp', scatter_dimension=0, tiled=True)  17.5 us
    all_to_all x1, waiting for transfers between devices, per_device(): lax.all_to_all(send_ga, 'dp', split_axis=0, concat_axis=0, tiled=True)  13.5 us
    unnamed x26, local copies, waits for them, and re-layouts  10.9 us
  transfers between devices with their start and end apart: 8, of which 8 were waited for; matrix products, arithmetic and copies ran while one was open for 11% of the time, Pallas kernels for 0%

profile of v1, /device:TPU:2, one launch (start us, length us, event | category | flops | bytes accessed | tf_op | source)
XLA Modules:
  0.0 371.6 jit_solution(4139565892914986625)
XLA Ops:
  7.2 1.0 select_reduce_fusion
  8.1 0.1 reduce_sum.32
  8.2 0.1 fusion.43
  8.4 0.1 fusion.18
  8.5 1.7 gather_fusion
  10.3 1.6 broadcast_select_fusion
  11.8 10.3 %all-to-all-start = ((bf16[32,512,64]{1,2,0:T(8,128)(2,1)}), bf16[32,512,64]{1,2,0:T(8,128)(2,1)}, u32[]{:S(2)}, u32[]{:S(2)}) async-start(bf16[32,512,64]{1,2,0:T(8,128)(2,1)} %broadcast_select_fusion), calls=%async_computation.1 | async-start | bytes 4194304 | tf_op jit(solution)/shard_map/all_to_all | solution.py:45
  22.1 0.0 all-gather.9.cloned.1.call-start
  22.2 27.9 %all-to-all-done = bf16[32,512,64]{1,2,0:T(8,128)(2,1)} async-done(((bf16[32,512,64]{1,2,0:T(8,128)(2,1)}), bf16[32,512,64]{1,2,0:T(8,128)(2,1)}, u32[]{:S(2)}, u32[]{:S(2)}) %all-to-all-start) | async-done | bytes 2097184 | tf_op jit(solution)/shard_map/all_to_all | solution.py:45
  50.1 2.2 gather_fusion.1
  52.3 1.2 convolution_bitcast_fusion
  53.6 0.0 all-gather.5.cloned.1.call-start
  53.6 0.7 all-gather.5.cloned.1.call-update
  54.3 0.0 reduce-scatter.2.cloned.1.call-start
  54.4 3.2 fusion.45
  57.6 0.0 reduce-scatter.2.cloned.1.call-update
  57.6 1.0 constant_dynamic-slice_fusion
  58.6 0.6 gather_fusion.2
  59.3 0.1 broadcast_select_fusion.1
  59.4 1.1 reshape.202
  60.5 5.9 %all-to-all-start.1 = ((bf16[32,2,2048]{2,1,0:T(2,128)(2,1)}), bf16[32,2,2048]{2,1,0:T(2,128)(2,1)S(1)}, u32[]{:S(2)}, u32[]{:S(2)}) async-start(bf16[32,2,2048]{2,1,0:T(2,128)(2,1)} %reshape.202), calls=%async_computation.2 | async-start | bytes 524288 | tf_op jit(solution)/shard_map/all_to_all | solution.py:46
  66.5 7.7 %all-to-all-done.1 = bf16[32,2,2048]{2,1,0:T(2,128)(2,1)S(1)} async-done(((bf16[32,2,2048]{2,1,0:T(2,128)(2,1)}), bf16[32,2,2048]{2,1,0:T(2,128)(2,1)S(1)}, u32[]{:S(2)}, u32[]{:S(2)}) %all-to-all-start.1) | async-done | bytes 262176 | tf_op jit(solution)/shard_map/all_to_all | solution.py:46
  74.2 0.4 reshape.203
  74.6 0.6 gather_fusion.3
  75.1 0.1 broadcast_select_fusion.6
  75.2 0.6 gather_fusion.4
  75.8 0.1 broadcast_select_fusion.3
  75.9 0.2 reshape.204
  76.2 27.9 %all_to_all.25 = bf16[16,2,2048]{2,1,0:T(2,128)(2,1)S(1)} all-to-all(bf16[16,2,2048]{2,1,0:T(2,128)(2,1)S(1)} %reshape.204), channel_id=1, replica_groups=mesh['dp'=32,'mp'=16] {'mp'}, dimensions={0} | all-to-all | bytes 262144 | tf_op jit(solution)/shard_map/all_to_all | solution.py:52
  104.1 0.2 reshape.205
  104.3 0.2 copy.46
  104.5 0.2 reshape.155
  104.7 0.2 fusion.8
  104.9 0.1 copy.47
  105.0 31.7 %all_gather.18 = bf16[1024,64]{1,0:T(8,128)(2,1)S(1)} all-gather(bf16[64,64]{1,0:T(8,128)(2,1)S(1)} %copy.47), channel_id=1, replica_groups=mesh['dp'=32,'mp'=16] {'mp'}, dimensions={0}, use_global_device_ids=true | all-gather | bytes 139264 | tf_op jit(solution)/shard_map/all_gather | solution.py:67
  136.6 0.8 all-gather.9.cloned.1.call-done
  137.4 2.5 reduce_sum.35
  140.0 68.8 %all-gather.5.cloned.1.call-done = bf16[1024,1024]{1,0:T(8,128)(2,1)} async-done(((bf16[64,1024]{1,0:T(8,128)(2,1)}), bf16[1024,1024]{1,0:T(8,128)(2,1)}) %all-gather.5.cloned.1.call-update) | async-done | bytes 2097168 | tf_op jit(solution)/shard_map/all_gather | solution.py:68
  208.8 1.2 fusion.13
  210.0 0.7 fusion.11
  210.7 0.6 copy.56
  211.3 1.4 reshape.206
  212.8 7.4 %all-to-all-start.4 = ((f32[32,1,4096]{2,1,0:T(1,128)}), f32[32,1,4096]{2,1,0:T(1,128)S(1)}, u32[]{:S(2)}, u32[]{:S(2)}) async-start(f32[32,1,4096]{2,1,0:T(1,128)} %reshape.206), calls=%async_computation.5 | async-start | bytes 1048576 | tf_op jit(solution)/shard_map/all_to_all | solution.py:91
  220.2 0.3 fusion.6
  220.5 0.8 convolution_convert_fusion
  221.4 2.5 copy.52
  223.9 6.8 %all-to-all-done.4 = f32[32,1,4096]{2,1,0:T(1,128)S(1)} async-done(((f32[32,1,4096]{2,1,0:T(1,128)}), f32[32,1,4096]{2,1,0:T(1,128)S(1)}, u32[]{:S(2)}, u32[]{:S(2)}) %all-to-all-start.4) | async-done | bytes 524320 | tf_op jit(solution)/shard_map/all_to_all | solution.py:91
  230.7 0.8 copy-done.3
  231.5 5.2 %all-to-all-start.3 = ((bf16[32,512,64]{1,2,0:T(8,128)(2,1)}), bf16[32,512,64]{1,2,0:T(8,128)(2,1)S(1)}, u32[]{:S(2)}, u32[]{:S(2)}) async-start(bf16[32,512,64]{1,2,0:T(8,128)(2,1)} %copy.52), calls=%async_computation.4 | async-start | bytes 4194304 | tf_op jit(solution)/shard_map/all_to_all | solution.py:90
  236.7 0.2 all-gather.7.cloned.1.call-start
  236.9 0.6 broadcast.234
  237.5 3.8 %reduce = f32[32,4096]{1,0:T(8,128)} reduce(f32[32,1,4096]{2,1,0:T(1,128)} %copy-done.3, f32[]{:T(128)} %broadcast.234), dimensions={1}, to_apply=%all_to_all.19.reduce_sub_computation | reduce | bytes 1048580 | tf_op jit(solution)/shard_map/all_to_all | solution.py:91
  241.2 2.4 reshape.207
  243.7 2.9 convolution_convert_fusion.2
  246.5 1.7 copy.58
  248.3 2.9 fusion.15
  251.2 13.5 %all-to-all-done.3 = bf16[32,512,64]{1,2,0:T(8,128)(2,1)S(1)} async-done(((bf16[32,512,64]{1,2,0:T(8,128)(2,1)}), bf16[32,512,64]{1,2,0:T(8,128)(2,1)S(1)}, u32[]{:S(2)}, u32[]{:S(2)}) %all-to-all-start.3) | async-done | bytes 2097184 | tf_op jit(solution)/shard_map/all_to_all | solution.py:90
  264.6 1.2 fusion.3
  265.9 1.0 copy.59
  266.8 3.9 %fusion = bf16[1024,512]{1,0:T(8,128)(2,1)} fusion(f32[8,128,512]{2,1,0:T(8,128)S(1)} %copy-done.2, bf16[1024,1024]{1,0:T(8,128)(2,1)} %all-gather.5.cloned.1.call-done, bf16[512,1024]{1,0:T(8,128)(2,1)S(1)} %copy-done.8), kind=kOutput, calls=%fused_computation.6 | convolution fusion | flops 1074790400 | bytes 6291456 | tf_op jit(solution)/shard_map/nc,dc->nd/dot_general | solution.py:69
  270.7 17.5 %reduce-scatter.2.cloned.1.call-done = f32[64,1024]{1,0:T(8,128)} async-done(((f32[1024,1024]{1,0:T(8,128)}), f32[64,1024]{1,0:T(8,128)}) %reduce-scatter.2.cloned.1.call-update) | async-done | bytes 262160 | tf_op jit(solution)/shard_map/reduce_scatter | solution.py:56
  288.3 1.9 fusion.7
  290.2 71.6 %all-gather.7.cloned.1.call-done = bf16[8,64,1024]{1,0,2:T(8,128)(2,1)} async-done(((bf16[8,64,64]{1,0,2:T(8,128)(2,1)}), bf16[8,64,1024]{1,0,2:T(8,128)(2,1)}) %all-gather.7.cloned.1.call-update) | async-done | bytes 1048592 | tf_op jit(solution)/shard_map/all_gather | solution.py:99
  361.8 3.3 copy.60
  (29 shorter events, 0.2 us)
Async XLA Ops:
  7.2 45.1 %copy-start = (bf16[1024,512]{1,0:T(8,128)(2,1)S(1)}, bf16[1024,512]{1,0:T(8,128)(2,1)}, u32[]{:S(2)}) copy-start(bf16[1024,512]{1,0:T(8,128)(2,1)} %param.7) | copy-start | bytes 3145732
  11.8 38.3 %all-to-all-start = ((bf16[32,512,64]{1,2,0:T(8,128)(2,1)}), bf16[32,512,64]{1,2,0:T(8,128)(2,1)}, u32[]{:S(2)}, u32[]{:S(2)}) async-start(bf16[32,512,64]{1,2,0:T(8,128)(2,1)} %broadcast_select_fusion), calls=%async_computation.1 | async-start | bytes 4194304 | tf_op jit(solution)/shard_map/all_to_all | solution.py:45
  22.1 115.3 %all-gather.9.cloned.1.call-start = ((), (), s32[]{:S(2)}) async-start(), calls=%async_computation.9 | async-start | bytes 4456448 | tf_op jit(solution)/shard_map/all_gather | solution.py:12
  22.2 32.2 %copy-start.7 = (bf16[512,1024]{1,0:T(8,128)(2,1)S(1)}, bf16[512,1024]{1,0:T(8,128)(2,1)}, u32[]{:S(2)}) copy-start(bf16[512,1024]{1,0:T(8,128)(2,1)} %param.8) | copy-start | bytes 3145732
  52.3 5.3 %copy-start.1 = (bf16[8,512,64]{1,2,0:T(8,128)(2,1)}, bf16[8,512,64]{1,2,0:T(8,128)(2,1)S(1)}, u32[]{:S(2)}) copy-start(bf16[8,512,64]{1,2,0:T(8,128)(2,1)S(1)} %gather_fusion.1) | copy-start | bytes 1572868
  53.6 155.2 %all-gather.5.cloned.1.call-start = ((), (), s32[]{:S(2)}) async-start(), calls=%async_computation.7 | async-start | bytes 2228224 | tf_op jit(solution)/shard_map/all_gather | solution.py:68
  54.3 234.0 %reduce-scatter.2.cloned.1.call-start = ((), (), s32[]{:S(2)}) async-start(), calls=%async_computation.6 | async-start | bytes 4456448 | tf_op jit(solution)/shard_map/reduce_scatter | solution.py:56
  60.5 13.7 %all-to-all-start.1 = ((bf16[32,2,2048]{2,1,0:T(2,128)(2,1)}), bf16[32,2,2048]{2,1,0:T(2,128)(2,1)S(1)}, u32[]{:S(2)}, u32[]{:S(2)}) async-start(bf16[32,2,2048]{2,1,0:T(2,128)(2,1)} %reshape.202), calls=%async_computation.2 | async-start | bytes 524288 | tf_op jit(solution)/shard_map/all_to_all | solution.py:46
  66.5 38.2 %copy-start.6 = (bf16[64,1024]{1,0:T(8,128)(2,1)S(1)}, bf16[64,1024]{1,0:T(8,128)(2,1)}, u32[]{:S(2)}) copy-start(bf16[64,1024]{1,0:T(8,128)(2,1)} %param.11) | copy-start | bytes 393220
  140.0 70.1 %copy-start.4 = (bf16[8,128,64]{1,2,0:T(8,128)(2,1)}, bf16[8,128,64]{1,2,0:T(8,128)(2,1)S(1)}, u32[]{:S(2)}) copy-start(bf16[8,128,64]{1,2,0:T(8,128)(2,1)S(1)} %reduce_sum.35) | copy-start | bytes 393220
  212.8 17.9 %all-to-all-start.4 = ((f32[32,1,4096]{2,1,0:T(1,128)}), f32[32,1,4096]{2,1,0:T(1,128)S(1)}, u32[]{:S(2)}, u32[]{:S(2)}) async-start(f32[32,1,4096]{2,1,0:T(1,128)} %reshape.206), calls=%async_computation.5 | async-start | bytes 1048576 | tf_op jit(solution)/shard_map/all_to_all | solution.py:91
  230.7 0.8 copy-start.3
  231.5 33.1 %all-to-all-start.3 = ((bf16[32,512,64]{1,2,0:T(8,128)(2,1)}), bf16[32,512,64]{1,2,0:T(8,128)(2,1)S(1)}, u32[]{:S(2)}, u32[]{:S(2)}) async-start(bf16[32,512,64]{1,2,0:T(8,128)(2,1)} %copy.52), calls=%async_computation.4 | async-start | bytes 4194304 | tf_op jit(solution)/shard_map/all_to_all | solution.py:90
  236.7 125.1 %all-gather.7.cloned.1.call-start = ((), (), s32[]{:S(2)}) async-start(), calls=%async_computation.8 | async-start | bytes 2228224 | tf_op jit(solution)/shard_map/all_gather | solution.py:99
  264.6 2.2 copy-start.2
  264.6 2.2 copy-start.8
  266.8 3.9 %copy-start.5 = (bf16[8,128,64]{1,2,0:T(8,128)(2,1)S(1)}, bf16[8,128,64]{1,2,0:T(8,128)(2,1)}, u32[]{:S(2)}) copy-start(bf16[8,128,64]{1,2,0:T(8,128)(2,1)} %copy-done.4) | copy-start | bytes 393220
Sparse Core Ops, SparseCore 0:
  53.7 83.6 all-gather.8
  139.5 69.2 all-gather.4
  211.6 76.5 reduce-scatter.1
  290.8 70.9 all-gather.6
